TPU v7x, 32 devices: a whole 2x2x4 slice. The times are simulated.
32 devices in a mesh: groups: 2 (over y), seq: 4 (over z), head: 2 (over x), sub: 2 (over core).
Axes of the slice: x: 2, y: 2, z: 4, core: 2. Of those that a mesh axis runs over, the one named last changes fastest.
Arguments:
- queries: bfloat16 [3072, 8192], P(('groups', 'seq', 'head', 'sub')), parts along dimension 0, may hold values from -128 to 128
- new_keys: bfloat16 [3072, 8192], P(('groups', 'seq', 'head', 'sub')), parts along dimension 0, may hold values from -4 to 4
- new_values: bfloat16 [3072, 8192], P(('groups', 'seq', 'head', 'sub')), parts along dimension 0, may hold values from -6 to 6
- key_cache: bfloat16 [2048, 8192], P(('groups', 'seq'), ('head', 'sub')), parts along dimension 0, may hold values from -6 to 6
- value_cache: bfloat16 [2048, 8192], P(('groups', 'seq'), ('head', 'sub')), parts along dimension 0, may hold values from -6 to 6
- selection: int32 [8, 2], P('groups'), parts along dimension 0, may hold values from 0 to 15, as said below
Outputs:
- attended: bfloat16 [3072, 8192], P(('groups', 'seq', 'head', 'sub')), parts along dimension 0
There are 2 independent parts, one for each index of `groups`. A program takes and returns all parts, laid end to end along the dimension named above; each array names one. Nothing has to cross between parts.
Inputs may be any that keep to these rules, and one draw needn't show every extreme that they name: `selection`: each row names 2 blocks that lie on 2 different indices of seq: the values block // 4 of a row are distinct. Every row names block 15.
All inputs are finite; a program needn't handle non-finite values.
Results may differ from a plain program's by a relative error of at most 0.0033.
Values may be sent and summed in bfloat16 or wider, within the bound.
No kernel may reach another device: no remote copies, remote signals or barrier semaphores. Data moves between devices by JAX's collectives and lax.ppermute only.
A program may use at most 64 MiB of HBM per device.

v0:
```python
import jax
import jax.numpy as jnp
from jax import lax
from jax.sharding import PartitionSpec as P

HD = 128
BLOCK = 64


def split_heads(rows_array, width):
    count = rows_array.shape[0]
    return rows_array.reshape(count, -1, width).transpose(1, 0, 2)


def per_device(queries, new_keys, new_values, key_cache, value_cache, selection):
    q_rows, k_rows, v_rows = (
        lax.all_to_all(queries, ("head", "sub"), split_axis=1, concat_axis=0, tiled=True),
        lax.all_to_all(new_keys, ("head", "sub"), split_axis=1, concat_axis=0, tiled=True),
        lax.all_to_all(new_values, ("head", "sub"), split_axis=1, concat_axis=0, tiled=True),
    )
    width = HD
    scale = float(width) ** (-0.5)
    q_heads = split_heads(q_rows, width)
    k_heads = split_heads(k_rows, width)
    v_heads = split_heads(v_rows, width)
    count = q_rows.shape[0]
    causal = lax.broadcasted_iota(jnp.int32, (count, count), 0) >= lax.broadcasted_iota(
        jnp.int32, (count, count), 1
    )

    def local_scores(pair):
        query_one, key_one = pair
        raw = jnp.dot(query_one, key_one.T, preferred_element_type=jnp.float32) * scale
        return jnp.where(causal, raw, jnp.float32(-1e30))

    me = lax.axis_index("seq")
    blk_dev = key_cache.shape[0] // BLOCK
    owner_of = selection // blk_dev
    matched = owner_of == me
    wanted = jnp.any(matched, axis=1)
    inner = jnp.sum(jnp.where(matched, selection % blk_dev, 0), axis=1)
    cache_k = key_cache.reshape(blk_dev, BLOCK, -1)
    cache_v = value_cache.reshape(blk_dev, BLOCK, -1)
    send_k = jnp.where(wanted[:, None, None], cache_k[inner], jnp.zeros((), jnp.bfloat16))
    send_v = jnp.where(wanted[:, None, None], cache_v[inner], jnp.zeros((), jnp.bfloat16))
    got_k, got_v = (
        lax.all_to_all(send_k, "seq", split_axis=0, concat_axis=0, tiled=True),
        lax.all_to_all(send_v, "seq", split_axis=0, concat_axis=0, tiled=True),
    )
    my_owners = lax.dynamic_index_in_dim(selection, me, 0, keepdims=False) // blk_dev
    fetched_k = split_heads(got_k[my_owners].reshape(-1, got_k.shape[2]), width)
    fetched_v = split_heads(got_v[my_owners].reshape(-1, got_v.shape[2]), width)

    def attend(query_one, value_one, remote_k, remote_v, own_scores):
        remote_scores = jnp.dot(query_one, remote_k.T, preferred_element_type=jnp.float32) * scale
        top = jnp.maximum(
            jnp.max(own_scores, axis=1, keepdims=True),
            jnp.max(remote_scores, axis=1, keepdims=True),
        )
        own_weights = jnp.exp(own_scores - top)
        remote_weights = jnp.exp(remote_scores - top)
        total = jnp.sum(own_weights, axis=1, keepdims=True) + jnp.sum(
            remote_weights, axis=1, keepdims=True
        )
        mixed = jnp.dot(
            own_weights.astype(jnp.bfloat16), value_one, preferred_element_type=jnp.float32
        )
        mixed = mixed + jnp.dot(
            remote_weights.astype(jnp.bfloat16), remote_v, preferred_element_type=jnp.float32
        )
        return (mixed / total).astype(jnp.bfloat16)

    def per_head(items):
        query_one, key_one, value_one, remote_k, remote_v = items
        return attend(query_one, value_one, remote_k, remote_v, local_scores((query_one, key_one)))

    result = lax.map(per_head, (q_heads, k_heads, v_heads, fetched_k, fetched_v))
    joined = result.transpose(1, 0, 2).reshape(count, -1)
    return lax.all_to_all(joined, ("head", "sub"), split_axis=0, concat_axis=1, tiled=True)


def solution(mesh):
    placed = (
        P(("groups", "seq", "head", "sub"), None),
        P(("groups", "seq", "head", "sub"), None),
        P(("groups", "seq", "head", "sub"), None),
        P(("groups", "seq"), ("head", "sub")),
        P(("groups", "seq"), ("head", "sub")),
        P("groups", None),
    )
    return jax.shard_map(
        per_device,
        mesh=mesh,
        in_specs=placed,
        out_specs=P(("groups", "seq", "head", "sub"), None),
        check_vma=False,
    )
```

profile of v0, /device:TPU:0, one launch (start us, length us, event | category | flops | bytes accessed | tf_op | source)
XLA Modules:
  0.0 226.7 jit_solution(10549713549970579454)
XLA Ops:
  0.0 2.8 %copy.40 = bf16[12,4,8,2048]{3,2,0,1:T(8,128)(2,1)} copy(bf16[12,4,8,2048]{3,2,1,0:T(8,128)(2,1)} %bitcast.118) | data formatting | bytes 3145728 | tf_op jit(solution)/shard_map/all_to_all | solution.py:17
  2.8 4.2 %all-to-all-start = ((bf16[96,4,2048]{2,0,1:T(8,128)(2,1)}), bf16[96,4,2048]{2,0,1:T(8,128)(2,1)S(1)}, u32[]{:S(2)}, u32[]{:S(2)}) async-start(bf16[96,4,2048]{2,0,1:T(8,128)(2,1)} %bitcast.109), calls=%async_computation | async-start | bytes 3145728 | tf_op jit(solution)/shard_map/all_to_all | solution.py:17
  7.1 2.7 %copy.39 = bf16[12,4,8,2048]{3,2,0,1:T(8,128)(2,1)} copy(bf16[12,4,8,2048]{3,2,1,0:T(8,128)(2,1)} %bitcast.119) | data formatting | bytes 3145728 | tf_op jit(solution)/shard_map/all_to_all | solution.py:18
  9.8 17.3 %all-to-all-done = bf16[96,4,2048]{2,0,1:T(8,128)(2,1)S(1)} async-done(((bf16[96,4,2048]{2,0,1:T(8,128)(2,1)}), bf16[96,4,2048]{2,0,1:T(8,128)(2,1)S(1)}, u32[]{:S(2)}, u32[]{:S(2)}) %all-to-all-start) | async-done | bytes 1572896 | tf_op jit(solution)/shard_map/all_to_all | solution.py:17
  27.1 4.3 %all-to-all-start.1 = ((bf16[96,4,2048]{2,0,1:T(8,128)(2,1)}), bf16[96,4,2048]{2,0,1:T(8,128)(2,1)}, u32[]{:S(2)}, u32[]{:S(2)}) async-start(bf16[96,4,2048]{2,0,1:T(8,128)(2,1)} %bitcast.108), calls=%async_computation.1 | async-start | bytes 3145728 | tf_op jit(solution)/shard_map/all_to_all | solution.py:18
  31.5 2.7 %copy.38 = bf16[12,4,8,2048]{3,2,0,1:T(8,128)(2,1)} copy(bf16[12,4,8,2048]{3,2,1,0:T(8,128)(2,1)} %bitcast.120) | data formatting | bytes 3145728 | tf_op jit(solution)/shard_map/all_to_all | solution.py:19
  34.2 17.4 %all-to-all-done.1 = bf16[96,4,2048]{2,0,1:T(8,128)(2,1)} async-done(((bf16[96,4,2048]{2,0,1:T(8,128)(2,1)}), bf16[96,4,2048]{2,0,1:T(8,128)(2,1)}, u32[]{:S(2)}, u32[]{:S(2)}) %all-to-all-start.1) | async-done | bytes 1572896 | tf_op jit(solution)/shard_map/all_to_all | solution.py:18
  51.6 4.5 %all-to-all-start.3 = ((bf16[96,4,2048]{2,0,1:T(8,128)(2,1)}), bf16[96,4,2048]{2,0,1:T(8,128)(2,1)}, u32[]{:S(2)}, u32[]{:S(2)}) async-start(bf16[96,4,2048]{2,0,1:T(8,128)(2,1)} %bitcast.107), calls=%async_computation.3 | async-start | bytes 3145728 | tf_op jit(solution)/shard_map/all_to_all | solution.py:19
  56.1 1.6 gather_fusion
  57.7 2.9 %gather_fusion.2 = bf16[4,64,2048]{2,1,0:T(8,128)(2,1)} fusion(bf16[4,64,2048]{2,1,0:T(8,128)(2,1)} %bitcast.121, s32[1024]{0:T(1024)S(1)} %pad_clamp_fusion.1), kind=kCustom, calls=%fused_computation.2 | custom fusion | bytes 2097168 | tf_op jit(solution)/shard_map/gather | solution.py:45
  60.6 3.1 %broadcast_select_fusion = (bf16[4,64,2048]{2,1,0:T(8,128)(2,1)}, bf16[4,64,2048]{2,1,0:T(8,128)(2,1)}) fusion(bf16[4,64,2048]{2,1,0:T(8,128)(2,1)} %gather_fusion.2, pred[4]{0:T(512)(128)(4,1)S(1)} %get-tuple-element.92, bf16[4,64,2048]{2,1,0:T(8,128)(2,1)} %gather_fusion), kind=kLoop, calls=%fused_computation.42 | loop fusion | flops 1048576 | bytes 4194308 | tf_op jit(solution)/shard_map/jit(_where)/select_n | solution.py:45
  63.7 12.5 %all-to-all-done.3 = bf16[96,4,2048]{2,0,1:T(8,128)(2,1)} async-done(((bf16[96,4,2048]{2,0,1:T(8,128)(2,1)}), bf16[96,4,2048]{2,0,1:T(8,128)(2,1)}, u32[]{:S(2)}, u32[]{:S(2)}) %all-to-all-start.3) | async-done | bytes 1572896 | tf_op jit(solution)/shard_map/all_to_all | solution.py:19
  76.2 31.2 %all_to_all.77 = bf16[4,64,2048]{2,1,0:T(8,128)(2,1)} all-to-all(bf16[4,64,2048]{2,1,0:T(8,128)(2,1)} %get-tuple-element.99), channel_id=1, replica_groups=mesh['groups'=2,'seq'=4,'head'=2,'sub'=2] {'seq'}, dimensions={0} | all-to-all | bytes 2097152 | tf_op jit(solution)/shard_map/all_to_all | solution.py:47
  107.3 4.3 %all-to-all-start.4 = ((bf16[4,64,2048]{2,1,0:T(8,128)(2,1)}), bf16[4,64,2048]{2,1,0:T(8,128)(2,1)}, u32[]{:S(2)}, u32[]{:S(2)}) async-start(bf16[4,64,2048]{2,1,0:T(8,128)(2,1)} %get-tuple-element.98), calls=%async_computation.4 | async-start | bytes 2097152 | tf_op jit(solution)/shard_map/all_to_all | solution.py:48
  112.2 1.6 copy.19
  113.8 1.8 copy.31
  115.6 1.6 copy.20
  117.2 1.8 copy.33
  119.4 1.8 gather_fusion.1
  122.3 14.1 %all-to-all-done.4 = bf16[4,64,2048]{2,1,0:T(8,128)(2,1)} async-done(((bf16[4,64,2048]{2,1,0:T(8,128)(2,1)}), bf16[4,64,2048]{2,1,0:T(8,128)(2,1)}, u32[]{:S(2)}, u32[]{:S(2)}) %all-to-all-start.4) | async-done | bytes 1048608 | tf_op jit(solution)/shard_map/all_to_all | solution.py:48
  136.4 1.8 gather_fusion.3
  138.5 58.9 %while.11 = (s32[]{:T(128)}, bf16[16,384,128]{2,1,0:T(8,128)(2,1)}, bf16[16,384,128]{2,1,0:T(8,128)(2,1)}, bf16[16,384,128]{2,1,0:T(8,128)(2,1)}, bf16[16,128,12...) while((s32[]{:T(128)}, bf16[16,384,128]{2,1,0:T(8,128)(2,1)}, ...), condition=%wide.region_7.8_spmd.clone, body=%wide.region_2.7_spmd.clone.sunk | while | flops 102284544 | bytes 3337305 | solution.py:77
  138.5 1.2 fusion.55
  142.2 1.2 fusion.55
  145.8 1.2 fusion.55
  147.0 1.1 fusion.56
  149.5 1.2 fusion.55
  153.2 1.2 fusion.55
  154.4 1.1 fusion.56
  156.9 1.2 fusion.55
  160.6 1.2 fusion.55
  161.8 1.1 fusion.56
  164.2 1.2 fusion.55
  167.9 1.2 fusion.55
  169.1 1.1 fusion.56
  171.6 1.2 fusion.55
  175.3 1.2 fusion.55
  176.5 1.1 fusion.56
  179.0 1.2 fusion.55
  182.6 1.2 fusion.55
  183.8 1.1 fusion.56
  186.3 1.2 fusion.55
  190.0 1.2 fusion.55
  193.7 1.2 fusion.55
  197.4 2.4 %copy.24 = bf16[384,16,128]{2,1,0:T(8,128)(2,1)S(1)} copy(bf16[384,16,128]{2,0,1:T(8,128)(2,1)} %bitcast.13) | data formatting | bytes 3145728 | tf_op jit(solution)/shard_map/transpose | solution.py:78
  199.8 2.1 all_to_all.67
  201.8 23.6 %all_to_all.78 = bf16[4,96,2048]{2,1,0:T(8,128)(2,1)S(1)} all-to-all(bf16[4,96,2048]{2,1,0:T(8,128)(2,1)} %all_to_all.67), channel_id=1, replica_groups=mesh['groups'=2,'seq'=4,'head'=2,'sub'=2] {'head','sub'}, dimensions={0} | all-to-all | bytes 3145728 | tf_op jit(solution)/shard_map/all_to_all | solution.py:79
  225.4 1.2 copy.29
  (124 shorter events, 35.1 us)
Async XLA Ops:
  0.0 56.1 %copy-start = (bf16[256,2048]{1,0:T(8,128)(2,1)S(1)}, bf16[256,2048]{1,0:T(8,128)(2,1)}, u32[]{:S(2)}) copy-start(bf16[256,2048]{1,0:T(8,128)(2,1)} %param.11) | copy-start | bytes 3145732
  2.8 24.3 %all-to-all-start = ((bf16[96,4,2048]{2,0,1:T(8,128)(2,1)}), bf16[96,4,2048]{2,0,1:T(8,128)(2,1)S(1)}, u32[]{:S(2)}, u32[]{:S(2)}) async-start(bf16[96,4,2048]{2,0,1:T(8,128)(2,1)} %bitcast.109), calls=%async_computation | async-start | bytes 3145728 | tf_op jit(solution)/shard_map/all_to_all | solution.py:17
  27.1 24.5 %all-to-all-start.1 = ((bf16[96,4,2048]{2,0,1:T(8,128)(2,1)}), bf16[96,4,2048]{2,0,1:T(8,128)(2,1)}, u32[]{:S(2)}, u32[]{:S(2)}) async-start(bf16[96,4,2048]{2,0,1:T(8,128)(2,1)} %bitcast.108), calls=%async_computation.1 | async-start | bytes 3145728 | tf_op jit(solution)/shard_map/all_to_all | solution.py:18
  51.6 4.5 %copy-start.1 = (s32[4,2]{0,1:T(2,128)S(1)}, s32[4,2]{0,1:T(2,128)}, u32[]{:S(2)}) copy-start(s32[4,2]{0,1:T(2,128)} %param.13) | copy-start | bytes 100
  51.6 24.6 %all-to-all-start.3 = ((bf16[96,4,2048]{2,0,1:T(8,128)(2,1)}), bf16[96,4,2048]{2,0,1:T(8,128)(2,1)}, u32[]{:S(2)}, u32[]{:S(2)}) async-start(bf16[96,4,2048]{2,0,1:T(8,128)(2,1)} %bitcast.107), calls=%async_computation.3 | async-start | bytes 3145728 | tf_op jit(solution)/shard_map/all_to_all | solution.py:19
  107.3 29.1 %all-to-all-start.4 = ((bf16[4,64,2048]{2,1,0:T(8,128)(2,1)}), bf16[4,64,2048]{2,1,0:T(8,128)(2,1)}, u32[]{:S(2)}, u32[]{:S(2)}) async-start(bf16[4,64,2048]{2,1,0:T(8,128)(2,1)} %get-tuple-element.98), calls=%async_computation.4 | async-start | bytes 2097152 | tf_op jit(solution)/shard_map/all_to_all | solution.py:48
where the time goes:
time: 229 us; the launch traced here: 227 us
  waiting for transfers between devices  61.3 us (27%)
  matrix products  55.4 us (24%)
  blocking collectives  54.8 us (24%)
  local copies, waits for them, and re-layouts  31.1 us (14%)
  starting transfers between devices  17.3 us (8%)
  other arithmetic  6.25 us (3%)
    all_to_all x1, blocking collectives, per_device(): lax.all_to_all(send_k, 'seq', split_axis=0, concat_axis=0, tiled=True)  31.2 us
    all_to_all x1, blocking collectives, per_device(): lax.all_to_all(joined, ('head', 'sub'), split_axis=0, concat_axis=1, tile...  23.6 us
    dot_general x16, matrix products, local_scores(): jnp.dot(query_one, key_one.T, preferred_element_type=jnp.float32) * scale  19.2 us
    dot_general x16, matrix products, attend(): jnp.dot(query_one, remote_k.T, preferred_element_type=jnp.float32) * scale  17.6 us
    all_to_all x1, waiting for transfers between devices, per_device(): lax.all_to_all(new_keys, ('head', 'sub'), split_axis=1, concat_axis=0, ti...  17.4 us
    all_to_all x1, waiting for transfers between devices, per_device(): lax.all_to_all(queries, ('head', 'sub'), split_axis=1, concat_axis=0, til...  17.3 us
    all_to_all x1, waiting for transfers between devices, per_device(): lax.all_to_all(send_v, 'seq', split_axis=0, concat_axis=0, tiled=True)  14.1 us
    dot_general x16, matrix products, attend(): jnp.dot(remote_weights.astype(jnp.bfloat16), remote_v, preferred_element_...  14 us
  transfers between devices with their start and end apart: 4, of which 4 were waited for; matrix products, arithmetic and copies ran while one was open for 10% of the time, Pallas kernels for 0%

commit v1 on v0

--- a/solution.py
+++ b/solution.py
@@ -5,6 +5,12 @@
 
 HD = 128
 BLOCK = 64
+
+
+def trade_parts(x, mesh_axis, split, join):
+    pieces = jnp.split(x, lax.axis_size(mesh_axis), axis=split)
+    received = lax.all_to_all(jnp.stack(pieces), mesh_axis, 0, 0)
+    return jnp.concatenate(received, axis=join)
 
 
 def split_heads(rows_array, width):
@@ -16,7 +22,7 @@
     q_rows, k_rows, v_rows = (
         lax.all_to_all(queries, ("head", "sub"), split_axis=1, concat_axis=0, tiled=True),
         lax.all_to_all(new_keys, ("head", "sub"), split_axis=1, concat_axis=0, tiled=True),
-        lax.all_to_all(new_values, ("head", "sub"), split_axis=1, concat_axis=0, tiled=True),
+        trade_parts(new_values, ("head", "sub"), 1, 0),
     )
     width = HD
     scale = float(width) ** (-0.5)

time: 229 us -> 229 us (level)
    all_to_all x1, waiting for transfers between devices: 17.4 us -> 12.5 us  [per_device(): lax.all_to_all(new_keys, ('head', 'sub'), split_axis=1, concat_axis=0, ti...]
    all_to_all x1, waiting for transfers between devices: 12.5 us -> 17.3 us  [trade_parts(): received = lax.all_to_all(jnp.stack(pieces), mesh_axis, 0, 0)]
    all_to_all x1 -> x0, local copies, waits for them, and re-layouts: 2.73 us -> none  [per_device(): lax.all_to_all(new_values, ('head', 'sub'), split_axis=1, concat_axis=0,...]
where the time goes in v1:
time: 229 us; the launch traced here: 227 us
  waiting for transfers between devices  61.3 us (27%)
  matrix products  55.4 us (24%)
  blocking collectives  54.8 us (24%)
  local copies, waits for them, and re-layouts  29.8 us (13%)
  starting transfers between devices  17.3 us (8%)
  other arithmetic  7.57 us (3%)
    all_to_all x1, blocking collectives, per_device(): lax.all_to_all(send_k, 'seq', split_axis=0, concat_axis=0, tiled=True)  31.2 us
    all_to_all x1, blocking collectives, per_device(): lax.all_to_all(joined, ('head', 'sub'), split_axis=0, concat_axis=1, tile...  23.6 us
    dot_general x16, matrix products, local_scores(): jnp.dot(query_one, key_one.T, preferred_element_type=jnp.float32) * scale  19.2 us
    dot_general x16, matrix products, attend(): jnp.dot(query_one, remote_k.T, preferred_element_type=jnp.float32) * scale  17.6 us
    all_to_all x1, waiting for transfers between devices, per_device(): lax.all_to_all(queries, ('head', 'sub'), split_axis=1, concat_axis=0, til...  17.4 us
    all_to_all x1, waiting for transfers between devices, trade_parts(): received = lax.all_to_all(jnp.stack(pieces), mesh_axis, 0, 0)  17.3 us
    all_to_all x1, waiting for transfers between devices, per_device(): lax.all_to_all(send_v, 'seq', split_axis=0, concat_axis=0, tiled=True)  14.1 us
    dot_general x16, matrix products, attend(): jnp.dot(remote_weights.astype(jnp.bfloat16), remote_v, preferred_element_...  14 us
  transfers between devices with their start and end apart: 4, of which 4 were waited for; matrix products, arithmetic and copies ran while one was open for 10% of the time, Pallas kernels for 0%

profile of v1, /device:TPU:0, one launch (start us, length us, event | category | flops | bytes accessed | tf_op | source)
XLA Modules:
  0.0 226.8 jit_solution(18228403921981456586)
XLA Ops:
  0.0 1.5 slice_bitcast_fusion.3
  1.6 1.4 pad_maximum_fusion
  2.9 4.2 %all-to-all-start.3 = ((bf16[4,96,2048]{2,1,0:T(8,128)(2,1)}), bf16[4,96,2048]{2,1,0:T(8,128)(2,1)S(1)}, u32[]{:S(2)}, u32[]{:S(2)}) async-start(bf16[4,96,2048]{2,1,0:T(8,128)(2,1)} %pad_maximum_fusion), calls=%async_computation.3 | async-start | bytes 3145728 | tf_op jit(solution)/shard_map/all_to_all | solution.py:12
  7.1 2.7 %copy.35 = bf16[12,4,8,2048]{3,2,0,1:T(8,128)(2,1)} copy(bf16[12,4,8,2048]{3,2,1,0:T(8,128)(2,1)} %bitcast.120) | data formatting | bytes 3145728 | tf_op jit(solution)/shard_map/all_to_all | solution.py:23
  9.9 17.3 %all-to-all-done.3 = bf16[4,96,2048]{2,1,0:T(8,128)(2,1)S(1)} async-done(((bf16[4,96,2048]{2,1,0:T(8,128)(2,1)}), bf16[4,96,2048]{2,1,0:T(8,128)(2,1)S(1)}, u32[]{:S(2)}, u32[]{:S(2)}) %all-to-all-start.3) | async-done | bytes 1572896 | tf_op jit(solution)/shard_map/all_to_all | solution.py:12
  27.2 4.3 %all-to-all-start = ((bf16[96,4,2048]{2,0,1:T(8,128)(2,1)}), bf16[96,4,2048]{2,0,1:T(8,128)(2,1)}, u32[]{:S(2)}, u32[]{:S(2)}) async-start(bf16[96,4,2048]{2,0,1:T(8,128)(2,1)} %bitcast.111), calls=%async_computation | async-start | bytes 3145728 | tf_op jit(solution)/shard_map/all_to_all | solution.py:23
  31.5 2.7 %copy.34 = bf16[12,4,8,2048]{3,2,0,1:T(8,128)(2,1)} copy(bf16[12,4,8,2048]{3,2,1,0:T(8,128)(2,1)} %bitcast.121) | data formatting | bytes 3145728 | tf_op jit(solution)/shard_map/all_to_all | solution.py:24
  34.3 17.4 %all-to-all-done = bf16[96,4,2048]{2,0,1:T(8,128)(2,1)} async-done(((bf16[96,4,2048]{2,0,1:T(8,128)(2,1)}), bf16[96,4,2048]{2,0,1:T(8,128)(2,1)}, u32[]{:S(2)}, u32[]{:S(2)}) %all-to-all-start) | async-done | bytes 1572896 | tf_op jit(solution)/shard_map/all_to_all | solution.py:23
  51.6 4.5 %all-to-all-start.1 = ((bf16[96,4,2048]{2,0,1:T(8,128)(2,1)}), bf16[96,4,2048]{2,0,1:T(8,128)(2,1)}, u32[]{:S(2)}, u32[]{:S(2)}) async-start(bf16[96,4,2048]{2,0,1:T(8,128)(2,1)} %bitcast.110), calls=%async_computation.1 | async-start | bytes 3145728 | tf_op jit(solution)/shard_map/all_to_all | solution.py:24
  56.2 1.6 gather_fusion
  57.8 2.8 %gather_fusion.2 = bf16[4,64,2048]{2,1,0:T(8,128)(2,1)} fusion(bf16[4,64,2048]{2,1,0:T(8,128)(2,1)} %bitcast.122, s32[1024]{0:T(1024)S(1)} %pad_clamp_fusion.1), kind=kCustom, calls=%fused_computation.2 | custom fusion | bytes 2097168 | tf_op jit(solution)/shard_map/gather | solution.py:51
  60.7 3.1 %broadcast_select_fusion = (bf16[4,64,2048]{2,1,0:T(8,128)(2,1)}, bf16[4,64,2048]{2,1,0:T(8,128)(2,1)}) fusion(bf16[4,64,2048]{2,1,0:T(8,128)(2,1)} %gather_fusion.2, pred[4]{0:T(512)(128)(4,1)S(1)} %get-tuple-element.92, bf16[4,64,2048]{2,1,0:T(8,128)(2,1)} %gather_fusion), kind=kLoop, calls=%fused_computation.42 | loop fusion | flops 1048576 | bytes 4194308 | tf_op jit(solution)/shard_map/jit(_where)/select_n | solution.py:51
  63.7 12.5 %all-to-all-done.1 = bf16[96,4,2048]{2,0,1:T(8,128)(2,1)} async-done(((bf16[96,4,2048]{2,0,1:T(8,128)(2,1)}), bf16[96,4,2048]{2,0,1:T(8,128)(2,1)}, u32[]{:S(2)}, u32[]{:S(2)}) %all-to-all-start.1) | async-done | bytes 1572896 | tf_op jit(solution)/shard_map/all_to_all | solution.py:24
  76.2 31.2 %all_to_all.66 = bf16[4,64,2048]{2,1,0:T(8,128)(2,1)} all-to-all(bf16[4,64,2048]{2,1,0:T(8,128)(2,1)} %get-tuple-element.103), channel_id=1, replica_groups=mesh['groups'=2,'seq'=4,'head'=2,'sub'=2] {'seq'}, dimensions={0} | all-to-all | bytes 2097152 | tf_op jit(solution)/shard_map/all_to_all | solution.py:53
  107.4 4.3 %all-to-all-start.4 = ((bf16[4,64,2048]{2,1,0:T(8,128)(2,1)}), bf16[4,64,2048]{2,1,0:T(8,128)(2,1)}, u32[]{:S(2)}, u32[]{:S(2)}) async-start(bf16[4,64,2048]{2,1,0:T(8,128)(2,1)} %get-tuple-element.102), calls=%async_computation.4 | async-start | bytes 2097152 | tf_op jit(solution)/shard_map/all_to_all | solution.py:54
  112.7 1.8 copy.27
  114.6 1.6 copy.17
  116.1 1.8 copy.28
  117.9 1.6 copy.18
  119.5 1.8 gather_fusion.1
  122.4 14.1 %all-to-all-done.4 = bf16[4,64,2048]{2,1,0:T(8,128)(2,1)} async-done(((bf16[4,64,2048]{2,1,0:T(8,128)(2,1)}), bf16[4,64,2048]{2,1,0:T(8,128)(2,1)}, u32[]{:S(2)}, u32[]{:S(2)}) %all-to-all-start.4) | async-done | bytes 1048608 | tf_op jit(solution)/shard_map/all_to_all | solution.py:54
  136.5 1.8 gather_fusion.3
  138.6 58.9 %while.11 = (s32[]{:T(128)}, bf16[16,384,128]{2,1,0:T(8,128)(2,1)}, bf16[16,384,128]{2,1,0:T(8,128)(2,1)}, bf16[16,384,128]{2,1,0:T(8,128)(2,1)}, bf16[16,128,12...) while((s32[]{:T(128)}, bf16[16,384,128]{2,1,0:T(8,128)(2,1)}, ...), condition=%wide.region_7.8_spmd.clone, body=%wide.region_2.7_spmd.clone.sunk | while | flops 102284544 | bytes 3337305 | solution.py:83
  138.6 1.2 fusion.55
  142.3 1.2 fusion.55
  143.5 1.1 fusion.56
  145.9 1.2 fusion.55
  147.1 1.1 fusion.56
  149.6 1.2 fusion.55
  150.8 1.1 fusion.56
  153.3 1.2 fusion.55
  157.0 1.2 fusion.55
  158.2 1.1 fusion.56
  160.7 1.2 fusion.55
  164.3 1.2 fusion.55
  165.5 1.1 fusion.56
  168.0 1.2 fusion.55
  171.7 1.2 fusion.55
  175.4 1.2 fusion.55
  179.1 1.2 fusion.55
  182.7 1.2 fusion.55
  186.4 1.2 fusion.55
  190.1 1.2 fusion.55
  193.8 1.2 fusion.55
  197.5 2.4 %copy.22 = bf16[384,16,128]{2,1,0:T(8,128)(2,1)S(1)} copy(bf16[384,16,128]{2,0,1:T(8,128)(2,1)} %bitcast.16) | data formatting | bytes 3145728 | tf_op jit(solution)/shard_map/transpose | solution.py:84
  199.9 2.1 all_to_all.56
  201.9 23.6 %all_to_all.67 = bf16[4,96,2048]{2,1,0:T(8,128)(2,1)S(1)} all-to-all(bf16[4,96,2048]{2,1,0:T(8,128)(2,1)} %all_to_all.56), channel_id=1, replica_groups=mesh['groups'=2,'seq'=4,'head'=2,'sub'=2] {'head','sub'}, dimensions={0} | all-to-all | bytes 3145728 | tf_op jit(solution)/shard_map/all_to_all | solution.py:85
  225.5 1.2 copy.26
  (125 shorter events, 36.2 us)
Async XLA Ops:
  0.0 56.2 %copy-start = (bf16[256,2048]{1,0:T(8,128)(2,1)S(1)}, bf16[256,2048]{1,0:T(8,128)(2,1)}, u32[]{:S(2)}) copy-start(bf16[256,2048]{1,0:T(8,128)(2,1)} %param.11) | copy-start | bytes 3145732
  2.9 24.3 %all-to-all-start.3 = ((bf16[4,96,2048]{2,1,0:T(8,128)(2,1)}), bf16[4,96,2048]{2,1,0:T(8,128)(2,1)S(1)}, u32[]{:S(2)}, u32[]{:S(2)}) async-start(bf16[4,96,2048]{2,1,0:T(8,128)(2,1)} %pad_maximum_fusion), calls=%async_computation.3 | async-start | bytes 3145728 | tf_op jit(solution)/shard_map/all_to_all | solution.py:12
  27.2 24.5 %all-to-all-start = ((bf16[96,4,2048]{2,0,1:T(8,128)(2,1)}), bf16[96,4,2048]{2,0,1:T(8,128)(2,1)}, u32[]{:S(2)}, u32[]{:S(2)}) async-start(bf16[96,4,2048]{2,0,1:T(8,128)(2,1)} %bitcast.111), calls=%async_computation | async-start | bytes 3145728 | tf_op jit(solution)/shard_map/all_to_all | solution.py:23
  51.6 4.5 %copy-start.1 = (s32[4,2]{0,1:T(2,128)S(1)}, s32[4,2]{0,1:T(2,128)}, u32[]{:S(2)}) copy-start(s32[4,2]{0,1:T(2,128)} %param.13) | copy-start | bytes 100
  51.6 24.6 %all-to-all-start.1 = ((bf16[96,4,2048]{2,0,1:T(8,128)(2,1)}), bf16[96,4,2048]{2,0,1:T(8,128)(2,1)}, u32[]{:S(2)}, u32[]{:S(2)}) async-start(bf16[96,4,2048]{2,0,1:T(8,128)(2,1)} %bitcast.110), calls=%async_computation.1 | async-start | bytes 3145728 | tf_op jit(solution)/shard_map/all_to_all | solution.py:24
  107.4 29.1 %all-to-all-start.4 = ((bf16[4,64,2048]{2,1,0:T(8,128)(2,1)}), bf16[4,64,2048]{2,1,0:T(8,128)(2,1)}, u32[]{:S(2)}, u32[]{:S(2)}) async-start(bf16[4,64,2048]{2,1,0:T(8,128)(2,1)} %get-tuple-element.102), calls=%async_computation.4 | async-start | bytes 2097152 | tf_op jit(solution)/shard_map/all_to_all | solution.py:54
